TPU v7x, 32 devices: a whole 2x2x4 slice. The times are simulated.
32 devices in a mesh: design: 2 (over y), layer: 4 (over z), harm: 4 (over x, core).
Axes of the slice: x: 2, y: 2, z: 4, core: 2. Of those that a mesh axis runs over, the one named last changes fastest.
Arguments:
- incident: float32 [2048, 512], P(('design', 'harm')), parts along dimension 0, may hold values from -6 to 6
- target: float32 [2048, 512], P(('design', 'harm')), parts along dimension 0, may hold values from -6 to 6
- down_diag: float32 [16, 1024, 128], P(('design', 'layer'), 'harm'), parts along dimension 0, may hold values from -0.375 to 0.375
- down_off: float32 [16, 1024, 128], P(('design', 'layer'), 'harm'), parts along dimension 0, may hold values from -0.375 to 0.375
- up_diag: float32 [16, 1024, 128], P(('design', 'layer'), 'harm'), parts along dimension 0, may hold values from -0.375 to 0.375
- up_off: float32 [16, 1024, 128], P(('design', 'layer'), 'harm'), parts along dimension 0, may hold values from -0.375 to 0.375
- design: float32 [16, 1024], P(('design', 'layer'), 'harm'), parts along dimension 0, may hold values from -0.5 to 0.5
- profile: float32 [16, 1024], replicated, may hold values from 0.25 to 1
- material: int32 [16], P(('design', 'layer')), parts along dimension 0, may hold values from 0 to 15
- offsets: int32 [16], P(('design', 'layer')), parts along dimension 0, may hold values from 1 to 7
Outputs:
- gradient: float32 [16, 1024], P(('design', 'layer'), 'harm'), parts along dimension 0
There are 2 independent parts, one for each index of `design`. A program takes and returns all parts, laid end to end along the dimension named above; an argument that names none is the same for every part. Nothing has to cross between parts.
All inputs are finite; a program needn't handle non-finite values.
Results may differ from a plain program's by a relative error of at most 0.00028.
Values sent between devices are 32-bit elements; how exact they have to be, the bound alone decides.
No kernel may reach another device: no remote copies, remote signals or barrier semaphores. Data moves between devices by JAX's collectives and lax.ppermute only.
A program may use at most 64 MiB of HBM per device.

v0:
```python
import jax
import jax.numpy as jnp
from jax import lax
from jax.sharding import PartitionSpec as P

precise = lax.Precision.HIGHEST


def passed_along(value, axis, steps):
    count = lax.axis_size(axis)
    first, last = (max(0, -steps), min(count, count - steps))
    return lax.ppermute(value, axis, [(source, source + steps) for source in range(first, last)])


def band_apply(diag_rows, off_rows, shift_by, field_in):
    block_size = diag_rows.shape[1]
    block_count = diag_rows.shape[0] // block_size
    col_width = field_in.shape[1]
    diag_blocks = diag_rows.reshape(block_count, block_size, block_size)
    off_blocks = off_rows.reshape(block_count, block_size, block_size)
    pieces_in = field_in.reshape(block_count, block_size, col_width)
    rolled = jnp.roll(pieces_in, -shift_by, axis=0)
    result = jnp.einsum("ijk,ikw->ijw", diag_blocks, pieces_in, precision=precise)
    result = result + jnp.einsum("ijk,ikw->ijw", off_blocks, rolled, precision=precise)
    return result.reshape(block_count * block_size, col_width)


def band_transpose(diag_rows, off_rows, shift_by, field_in):
    block_size = diag_rows.shape[1]
    block_count = diag_rows.shape[0] // block_size
    col_width = field_in.shape[1]
    diag_blocks = diag_rows.reshape(block_count, block_size, block_size)
    off_blocks = off_rows.reshape(block_count, block_size, block_size)
    pieces_in = field_in.reshape(block_count, block_size, col_width)
    result = jnp.einsum("ikj,ikw->ijw", diag_blocks, pieces_in, precision=precise)
    spread = jnp.einsum("ikj,ikw->ijw", off_blocks, pieces_in, precision=precise)
    result = result + jnp.roll(spread, shift_by, axis=0)
    return result.reshape(block_count * block_size, col_width)


def run_line(entry_field, local_fn, passer, is_first, turn_count, col_width):

    def one_turn(turn_idx, carried):
        result, _ = local_fn(carried, 0, col_width)
        return jnp.where(is_first, entry_field, passer(result))

    start_field = jnp.where(is_first, entry_field, jnp.zeros_like(entry_field))
    carried = lax.fori_loop(0, turn_count - 1, one_turn, start_field)
    return local_fn(carried, 0, col_width)[1]


def body(
    incident, target, down_diag, down_off, up_diag, up_off, design, profile, material, offsets
):
    columns, aim_cols = (
        lax.all_to_all(incident, "harm", split_axis=1, concat_axis=0, tiled=True),
        lax.all_to_all(target, "harm", split_axis=1, concat_axis=0, tiled=True),
    )
    down_full, down_side, up_full, up_side, design_full = (
        lax.all_gather(down_diag, "harm", axis=1, tiled=True),
        lax.all_gather(down_off, "harm", axis=1, tiled=True),
        lax.all_gather(up_diag, "harm", axis=1, tiled=True),
        lax.all_gather(up_off, "harm", axis=1, tiled=True),
        lax.all_gather(design, "harm", axis=1, tiled=True),
    )
    onehot = (material[:, None] == jnp.arange(profile.shape[0], dtype=jnp.int32)[None, :]).astype(
        jnp.float32
    )
    shape_rows = jnp.dot(onehot, profile, precision=precise)
    reflect = design_full * shape_rows
    col_width = columns.shape[1]
    total_inc = col_width * lax.axis_size("harm")
    layer_count = lax.axis_size("layer")
    where_now = lax.axis_index("layer")

    def down_local(source, col_start, span_width):

        def down_step(carried, layer_in):
            diag_rows, off_rows, shift_by = layer_in
            return (band_apply(diag_rows, off_rows, shift_by, carried), carried)

        result, stacked = lax.scan(down_step, source, (down_full, down_side, offsets))
        return (result, stacked)

    down_stack = run_line(
        columns,
        down_local,
        lambda sent: passed_along(sent, "layer", 1),
        where_now == 0,
        layer_count,
        col_width,
    )

    def up_local(source, col_start, span_width):

        def up_step(carried, layer_in):
            diag_rows, off_rows, shift_by, reflect_row, down_here = layer_in
            return (
                reflect_row[:, None] * down_here
                + band_apply(diag_rows, off_rows, shift_by, carried),
                None,
            )

        result, _ = lax.scan(
            up_step, source, (up_full, up_side, offsets, reflect, down_stack), reverse=True
        )
        return (result, result)

    def adjoint_local(source, col_start, span_width):

        def adjoint_step(carried, layer_in):
            diag_rows, off_rows, shift_by = layer_in
            return (band_transpose(diag_rows, off_rows, shift_by, carried), carried)

        result, stacked = lax.scan(adjoint_step, source, (up_full, up_side, offsets))
        return (result, stacked)

    zero_cols = jnp.zeros_like(columns)
    reflected = run_line(
        zero_cols,
        up_local,
        lambda sent: passed_along(sent, "layer", -1),
        where_now == layer_count - 1,
        layer_count,
        col_width,
    )
    adjoint_start = (reflected - aim_cols) / total_inc
    adjoint_stack = run_line(
        adjoint_start,
        adjoint_local,
        lambda sent: passed_along(sent, "layer", 1),
        where_now == 0,
        layer_count,
        col_width,
    )
    partial_terms = jnp.sum(adjoint_stack * down_stack, axis=2) * shape_rows
    return lax.psum_scatter(partial_terms, "harm", scatter_dimension=1, tiled=True)


def solution(mesh):
    return jax.shard_map(
        body,
        mesh=mesh,
        in_specs=(
            P(("design", "harm"), None),
            P(("design", "harm"), None),
            P(("design", "layer"), "harm", None),
            P(("design", "layer"), "harm", None),
            P(("design", "layer"), "harm", None),
            P(("design", "layer"), "harm", None),
            P(("design", "layer"), "harm"),
            P(),
            P(("design", "layer")),
            P(("design", "layer")),
        ),
        out_specs=P(("design", "layer"), "harm"),
        check_vma=False,
    )
```

profile of v0, /device:TPU:0, one launch (start us, length us, event | category | flops | bytes accessed | tf_op | source)
XLA Modules:
  0.0 318.8 jit_solution(7895070992291923080)
XLA Ops:
  9.6 4.4 %all-to-all-start = ((f32[256,4,128]{2,0,1:T(8,128)}), f32[256,4,128]{2,0,1:T(8,128)S(1)}, u32[]{:S(2)}, u32[]{:S(2)}) async-start(f32[256,4,128]{2,0,1:T(8,128)} %copy_bitcast_fusion.1), calls=%async_computation | async-start | bytes 1048576 | tf_op jit(solution)/shard_map/all_to_all | solution.py:56
  15.2 10.8 %all_gather.15 = f32[2,1024]{1,0:T(2,128)S(1)} all-gather(f32[2,256]{1,0:T(2,128)S(1)} %copy-done.11), channel_id=1, replica_groups=mesh['design'=2,'layer'=4,'harm'=4] {'harm'}, dimensions={1}, use_global_device_ids=true | all-gather | bytes 10240 | tf_op jit(solution)/shard_map/all_gather | solution.py:64
  28.3 4.1 %all-to-all-start.1 = ((f32[256,4,128]{2,0,1:T(8,128)}), f32[256,4,128]{2,0,1:T(8,128)}, u32[]{:S(2)}, u32[]{:S(2)}) async-start(f32[256,4,128]{2,0,1:T(8,128)} %copy_bitcast_fusion), calls=%async_computation.1 | async-start | bytes 1048576 | tf_op jit(solution)/shard_map/all_to_all | solution.py:57
  32.6 16.6 %all-gather.7.cloned.1.call-done = f32[2,1024,128]{2,1,0:T(8,128)} async-done(((f32[2,256,128]{2,1,0:T(8,128)}), f32[2,1024,128]{2,1,0:T(8,128)}) %all-gather.7.cloned.1.call-update) | async-done | bytes 1048592 | tf_op jit(solution)/shard_map/all_gather | solution.py:61
  49.2 69.4 %while.121 = (s32[]{:T(128)}, f32[1024,128]{1,0:T(8,128)S(1)}, pred[]{:T(512)}, f32[2,1024,128]{2,1,0:T(8,128)}, f32[2,1024,128]{2,1,0:T(8,128)}, /*index=5*/s32...) while((s32[]{:T(128)}, f32[1024,128]{1,0:T(8,128)S(1)}, ...), condition=%wide.region_3.5_spmd, body=%wide.region_0.4_spmd.sunk | while | flops 403046400 | bytes 10486314 | solution.py:48
  49.2 8.1 %while.129 = (s32[]{:T(128)}, f32[1024,128]{1,0:T(8,128)S(1)}, f32[2,1024,128]{2,1,0:T(8,128)}, f32[2,1024,128]{2,1,0:T(8,128)}, s32[2]{0:T(128)S(1)}, /*index=5...) while((s32[]{:T(128)}, f32[1024,128]{1,0:T(8,128)S(1)}, f32[2,1024,128]{2,1,0:T(8,128)}, ...), condition=%wide.region_2.3_spmd, body=%wide.region_1.2_spmd.sunk | while | flops 402915328 | bytes 6816028 | solution.py:82
  50.6 1.3 constant_dynamic-slice_fusion.29
  54.7 1.3 constant_dynamic-slice_fusion.29
  57.3 4.0 %collective-permute-start.2 = (f32[1024,128]{1,0:T(8,128)S(1)}, f32[1024,128]{1,0:T(8,128)S(1)}, u32[]{:S(2)}, u32[]{:S(2)}) collective-permute-start(f32[1024,128]{1,0:T(8,128)S(1)} %get-tuple-element.1181), channel_id=1, source_target_pairs={{0,4},{4,8},{8,12},{1,5},{5,9},{9,13},{2,6},{6,10},{10,14},{3,7},{... | collective-permute-start | bytes 1572872 | tf_op jit(solution)/shard_map/while/body/eval_jaxpr/ppermute | solution.py:12
  61.3 11.5 %collective-permute-done.2 = f32[1024,128]{1,0:T(8,128)S(1)} collective-permute-done((f32[1024,128]{1,0:T(8,128)S(1)}, f32[1024,128]{1,0:T(8,128)S(1)}, u32[]{:S(2)}, u32[]{:S(2)}) %collective-permute-start.2) | collective-permute-done | bytes 524320 | tf_op jit(solution)/shard_map/while/body/eval_jaxpr/ppermute | solution.py:12
  72.9 8.1 %while.129 = (s32[]{:T(128)}, f32[1024,128]{1,0:T(8,128)S(1)}, f32[2,1024,128]{2,1,0:T(8,128)}, f32[2,1024,128]{2,1,0:T(8,128)}, s32[2]{0:T(128)S(1)}, /*index=5...) while((s32[]{:T(128)}, f32[1024,128]{1,0:T(8,128)S(1)}, f32[2,1024,128]{2,1,0:T(8,128)}, ...), condition=%wide.region_2.3_spmd, body=%wide.region_1.2_spmd.sunk | while | flops 402915328 | bytes 6816028 | solution.py:82
  74.3 1.3 constant_dynamic-slice_fusion.29
  78.4 1.3 constant_dynamic-slice_fusion.29
  81.0 4.4 %collective-permute-start.2 = (f32[1024,128]{1,0:T(8,128)S(1)}, f32[1024,128]{1,0:T(8,128)S(1)}, u32[]{:S(2)}, u32[]{:S(2)}) collective-permute-start(f32[1024,128]{1,0:T(8,128)S(1)} %get-tuple-element.1181), channel_id=1, source_target_pairs={{0,4},{4,8},{8,12},{1,5},{5,9},{9,13},{2,6},{6,10},{10,14},{3,7},{... | collective-permute-start | bytes 1572872 | tf_op jit(solution)/shard_map/while/body/eval_jaxpr/ppermute | solution.py:12
  85.5 10.6 %collective-permute-done.2 = f32[1024,128]{1,0:T(8,128)S(1)} collective-permute-done((f32[1024,128]{1,0:T(8,128)S(1)}, f32[1024,128]{1,0:T(8,128)S(1)}, u32[]{:S(2)}, u32[]{:S(2)}) %collective-permute-start.2) | collective-permute-done | bytes 524320 | tf_op jit(solution)/shard_map/while/body/eval_jaxpr/ppermute | solution.py:12
  96.2 8.1 %while.129 = (s32[]{:T(128)}, f32[1024,128]{1,0:T(8,128)S(1)}, f32[2,1024,128]{2,1,0:T(8,128)}, f32[2,1024,128]{2,1,0:T(8,128)}, s32[2]{0:T(128)S(1)}, /*index=5...) while((s32[]{:T(128)}, f32[1024,128]{1,0:T(8,128)S(1)}, f32[2,1024,128]{2,1,0:T(8,128)}, ...), condition=%wide.region_2.3_spmd, body=%wide.region_1.2_spmd.sunk | while | flops 402915328 | bytes 6816028 | solution.py:82
  97.6 1.3 constant_dynamic-slice_fusion.29
  101.7 1.3 constant_dynamic-slice_fusion.29
  104.3 4.4 %collective-permute-start.2 = (f32[1024,128]{1,0:T(8,128)S(1)}, f32[1024,128]{1,0:T(8,128)S(1)}, u32[]{:S(2)}, u32[]{:S(2)}) collective-permute-start(f32[1024,128]{1,0:T(8,128)S(1)} %get-tuple-element.1181), channel_id=1, source_target_pairs={{0,4},{4,8},{8,12},{1,5},{5,9},{9,13},{2,6},{6,10},{10,14},{3,7},{... | collective-permute-start | bytes 1572872 | tf_op jit(solution)/shard_map/while/body/eval_jaxpr/ppermute | solution.py:12
  108.8 9.8 %collective-permute-done.2 = f32[1024,128]{1,0:T(8,128)S(1)} collective-permute-done((f32[1024,128]{1,0:T(8,128)S(1)}, f32[1024,128]{1,0:T(8,128)S(1)}, u32[]{:S(2)}, u32[]{:S(2)}) %collective-permute-start.2) | collective-permute-done | bytes 524320 | tf_op jit(solution)/shard_map/while/body/eval_jaxpr/ppermute | solution.py:12
  118.7 1.1 copy-done.5
  119.8 7.9 %while.122 = (s32[]{:T(128)}, f32[1024,128]{1,0:T(8,128)S(1)}, f32[2,1024,128]{2,1,0:T(8,128)S(1)}, f32[2,1024,128]{2,1,0:T(8,128)}, f32[2,1024,128]{2,1,0:T(8,1...) while((s32[]{:T(128)}, f32[1024,128]{1,0:T(8,128)S(1)}, ...), condition=%wide.region_5.7_spmd, body=%wide.region_4.6_spmd.sunk | while | flops 402915328 | bytes 12058948 | solution.py:82
  121.2 1.1 copy-done.6
  125.1 1.1 copy-done.6
  127.8 69.0 %while.128 = (s32[]{:T(128)}, f32[1024,128]{1,0:T(8,128)}, pred[]{:T(512)}, f32[2,1024]{1,0:T(2,128)S(1)}, f32[2,1024,128]{2,1,0:T(8,128)S(1)}, /*index=5*/f32[2...) while((s32[]{:T(128)}, f32[1024,128]{1,0:T(8,128)}, ...), condition=%wide.region_9.11_spmd.clone, body=%wide.region_6.10_spmd.clone.sunk | while | flops 403439616 | bytes 15741572 | solution.py:48
  127.9 1.2 copy-done.1
  129.0 7.9 %while.131 = (s32[]{:T(128)}, f32[1024,128]{1,0:T(8,128)S(1)}, f32[2,1024]{1,0:T(2,128)S(1)}, f32[2,1024,128]{2,1,0:T(8,128)S(1)}, f32[2,1024,128]{2,1,0:T(8,128...) while((s32[]{:T(128)}, f32[1024,128]{1,0:T(8,128)S(1)}, ...), condition=%wide.region_8.9_spmd, body=%wide.region_7.8_spmd.sunk | while | flops 403177472 | bytes 7352640 | solution.py:104
  130.3 1.1 constant_dynamic-slice_fusion.26
  134.2 1.1 constant_dynamic-slice_fusion.26
  136.9 1.3 collective-permute-start
  138.2 12.8 %collective-permute-done = f32[1024,128]{1,0:T(8,128)S(1)} collective-permute-done((f32[1024,128]{1,0:T(8,128)S(1)}, f32[1024,128]{1,0:T(8,128)S(1)}, u32[]{:S(2)}, u32[]{:S(2)}) %collective-permute-start) | collective-permute-done | bytes 524320 | tf_op jit(solution)/shard_map/while/body/eval_jaxpr/ppermute | solution.py:12
  151.9 1.2 broadcast_select_fusion.12
  153.2 7.9 %while.131 = (s32[]{:T(128)}, f32[1024,128]{1,0:T(8,128)S(1)}, f32[2,1024]{1,0:T(2,128)S(1)}, f32[2,1024,128]{2,1,0:T(8,128)S(1)}, f32[2,1024,128]{2,1,0:T(8,128...) while((s32[]{:T(128)}, f32[1024,128]{1,0:T(8,128)S(1)}, ...), condition=%wide.region_8.9_spmd, body=%wide.region_7.8_spmd.sunk | while | flops 403177472 | bytes 7352640 | solution.py:104
  154.5 1.1 constant_dynamic-slice_fusion.26
  158.4 1.1 constant_dynamic-slice_fusion.26
  161.1 1.3 collective-permute-start
  162.4 11.5 %collective-permute-done = f32[1024,128]{1,0:T(8,128)S(1)} collective-permute-done((f32[1024,128]{1,0:T(8,128)S(1)}, f32[1024,128]{1,0:T(8,128)S(1)}, u32[]{:S(2)}, u32[]{:S(2)}) %collective-permute-start) | collective-permute-done | bytes 524320 | tf_op jit(solution)/shard_map/while/body/eval_jaxpr/ppermute | solution.py:12
  174.8 1.2 broadcast_select_fusion.12
  176.1 7.9 %while.131 = (s32[]{:T(128)}, f32[1024,128]{1,0:T(8,128)S(1)}, f32[2,1024]{1,0:T(2,128)S(1)}, f32[2,1024,128]{2,1,0:T(8,128)S(1)}, f32[2,1024,128]{2,1,0:T(8,128...) while((s32[]{:T(128)}, f32[1024,128]{1,0:T(8,128)S(1)}, ...), condition=%wide.region_8.9_spmd, body=%wide.region_7.8_spmd.sunk | while | flops 403177472 | bytes 7352640 | solution.py:104
  177.4 1.1 constant_dynamic-slice_fusion.26
  181.3 1.1 constant_dynamic-slice_fusion.26
  184.1 1.3 collective-permute-start
  185.4 10.6 %collective-permute-done = f32[1024,128]{1,0:T(8,128)S(1)} collective-permute-done((f32[1024,128]{1,0:T(8,128)S(1)}, f32[1024,128]{1,0:T(8,128)S(1)}, u32[]{:S(2)}, u32[]{:S(2)}) %collective-permute-start) | collective-permute-done | bytes 524320 | tf_op jit(solution)/shard_map/while/body/eval_jaxpr/ppermute | solution.py:12
  196.8 10.2 %while.123 = (s32[]{:T(128)}, f32[1024,128]{1,0:T(8,128)}, f32[2,1024]{1,0:T(2,128)S(1)}, f32[2,1024,128]{2,1,0:T(8,128)S(1)}, f32[2,1024,128]{2,1,0:T(8,128)}, ...) while((s32[]{:T(128)}, f32[1024,128]{1,0:T(8,128)}, ...), condition=%wide.region_11.13_spmd, body=%wide.region_10.12_spmd.sunk | while | flops 403177472 | bytes 9449820 | solution.py:104
  198.2 1.3 constant_dynamic-slice_fusion.23
  203.2 1.3 constant_dynamic-slice_fusion.23
  208.0 2.2 broadcast_select_fusion.4
  210.2 63.5 %while.125 = (s32[]{:T(128)}, f32[1024,128]{1,0:T(8,128)S(1)}, pred[]{:T(512)}, f32[2,1024,128]{2,1,0:T(8,128)S(1)}, f32[2,1024,128]{2,1,0:T(8,128)S(1)}, /*inde...) while((s32[]{:T(128)}, f32[1024,128]{1,0:T(8,128)S(1)}, ...), condition=%wide.region_15.17_spmd, body=%wide.region_12.16_spmd.sunk | while | flops 403046400 | bytes 10486314 | solution.py:48
  210.2 9.3 %while.130 = (s32[]{:T(128)}, f32[1024,128]{1,0:T(8,128)S(1)}, f32[2,1024,128]{2,1,0:T(8,128)S(1)}, f32[2,1024,128]{2,1,0:T(8,128)S(1)}, s32[2]{0:T(128)S(1)}, /...) while((s32[]{:T(128)}, f32[1024,128]{1,0:T(8,128)S(1)}, f32[2,1024,128]{2,1,0:T(8,128)S(1)}, ...), condition=%wide.region_14.15_spmd, body=%wide.region_13.14_spmd.sunk | while | flops 402915328 | bytes 6816020 | solution.py:115
  219.5 3.9 %collective-permute-start.1 = (f32[1024,128]{1,0:T(8,128)S(1)}, f32[1024,128]{1,0:T(8,128)}, u32[]{:S(2)}, u32[]{:S(2)}) collective-permute-start(f32[1024,128]{1,0:T(8,128)S(1)} %get-tuple-element.1207), channel_id=1, source_target_pairs={{0,4},{4,8},{8,12},{1,5},{5,9},{9,13},{2,6},{6,10},{10,14},{3,7},{... | collective-permute-start | bytes 1572872 | tf_op jit(solution)/shard_map/while/body/eval_jaxpr/ppermute | solution.py:12
  223.4 5.9 %collective-permute-done.1 = f32[1024,128]{1,0:T(8,128)} collective-permute-done((f32[1024,128]{1,0:T(8,128)S(1)}, f32[1024,128]{1,0:T(8,128)}, u32[]{:S(2)}, u32[]{:S(2)}) %collective-permute-start.1) | collective-permute-done | bytes 524320 | tf_op jit(solution)/shard_map/while/body/eval_jaxpr/ppermute | solution.py:12
  229.3 1.1 broadcast_select_fusion.11
  230.4 9.3 %while.130 = (s32[]{:T(128)}, f32[1024,128]{1,0:T(8,128)S(1)}, f32[2,1024,128]{2,1,0:T(8,128)S(1)}, f32[2,1024,128]{2,1,0:T(8,128)S(1)}, s32[2]{0:T(128)S(1)}, /...) while((s32[]{:T(128)}, f32[1024,128]{1,0:T(8,128)S(1)}, f32[2,1024,128]{2,1,0:T(8,128)S(1)}, ...), condition=%wide.region_14.15_spmd, body=%wide.region_13.14_spmd.sunk | while | flops 402915328 | bytes 6816020 | solution.py:115
  239.8 5.3 %collective-permute-start.1 = (f32[1024,128]{1,0:T(8,128)S(1)}, f32[1024,128]{1,0:T(8,128)}, u32[]{:S(2)}, u32[]{:S(2)}) collective-permute-start(f32[1024,128]{1,0:T(8,128)S(1)} %get-tuple-element.1207), channel_id=1, source_target_pairs={{0,4},{4,8},{8,12},{1,5},{5,9},{9,13},{2,6},{6,10},{10,14},{3,7},{... | collective-permute-start | bytes 1572872 | tf_op jit(solution)/shard_map/while/body/eval_jaxpr/ppermute | solution.py:12
  245.1 5.9 %collective-permute-done.1 = f32[1024,128]{1,0:T(8,128)} collective-permute-done((f32[1024,128]{1,0:T(8,128)S(1)}, f32[1024,128]{1,0:T(8,128)}, u32[]{:S(2)}, u32[]{:S(2)}) %collective-permute-start.1) | collective-permute-done | bytes 524320 | tf_op jit(solution)/shard_map/while/body/eval_jaxpr/ppermute | solution.py:12
  250.9 1.1 broadcast_select_fusion.11
  252.1 9.3 %while.130 = (s32[]{:T(128)}, f32[1024,128]{1,0:T(8,128)S(1)}, f32[2,1024,128]{2,1,0:T(8,128)S(1)}, f32[2,1024,128]{2,1,0:T(8,128)S(1)}, s32[2]{0:T(128)S(1)}, /...) while((s32[]{:T(128)}, f32[1024,128]{1,0:T(8,128)S(1)}, f32[2,1024,128]{2,1,0:T(8,128)S(1)}, ...), condition=%wide.region_14.15_spmd, body=%wide.region_13.14_spmd.sunk | while | flops 402915328 | bytes 6816020 | solution.py:115
  261.4 5.3 %collective-permute-start.1 = (f32[1024,128]{1,0:T(8,128)S(1)}, f32[1024,128]{1,0:T(8,128)}, u32[]{:S(2)}, u32[]{:S(2)}) collective-permute-start(f32[1024,128]{1,0:T(8,128)S(1)} %get-tuple-element.1207), channel_id=1, source_target_pairs={{0,4},{4,8},{8,12},{1,5},{5,9},{9,13},{2,6},{6,10},{10,14},{3,7},{... | collective-permute-start | bytes 1572872 | tf_op jit(solution)/shard_map/while/body/eval_jaxpr/ppermute | solution.py:12
  266.7 5.9 %collective-permute-done.1 = f32[1024,128]{1,0:T(8,128)} collective-permute-done((f32[1024,128]{1,0:T(8,128)S(1)}, f32[1024,128]{1,0:T(8,128)}, u32[]{:S(2)}, u32[]{:S(2)}) %collective-permute-start.1) | collective-permute-done | bytes 524320 | tf_op jit(solution)/shard_map/while/body/eval_jaxpr/ppermute | solution.py:12
  272.6 1.1 broadcast_select_fusion.11
  274.8 10.7 %while.126 = (s32[]{:T(128)}, f32[1024,128]{1,0:T(8,128)S(1)}, f32[2,1024,128]{2,1,0:T(8,128)}, f32[2,1024,128]{2,1,0:T(8,128)S(1)}, f32[2,1024,128]{2,1,0:T(8,1...) while((s32[]{:T(128)}, f32[1024,128]{1,0:T(8,128)S(1)}, ...), condition=%wide.region_17.19_spmd, body=%wide.region_16.18_spmd.sunk | while | flops 402915328 | bytes 7865116 | solution.py:115
  285.5 1.9 multiply_reduce_fusion
  288.5 22.2 %reduce-scatter.4.cloned.1.call-done = f32[256,2]{1,0:T(8,128)} async-done(((f32[1024,2]{1,0:T(8,128)}), f32[256,2]{1,0:T(8,128)}) %reduce-scatter.4.cloned.1.call-update) | async-done | bytes 2064
  310.7 1.6 copy.30
  (181 shorter events, 72.0 us)
Async XLA Ops:
  6.5 2.2 copy-start
  6.5 26.1 %all-gather.5.cloned.1.call-start = ((), (), s32[]{:S(2)}) async-start(), calls=%async_computation.3 | async-start | bytes 1310720 | tf_op jit(solution)/shard_map/all_gather | solution.py:60
  7.3 42.0 %all-gather.7.cloned.1.call-start = ((), (), s32[]{:S(2)}) async-start(), calls=%async_computation.4 | async-start | bytes 1310720 | tf_op jit(solution)/shard_map/all_gather | solution.py:61
  8.0 119.7 %all-gather.11.cloned.1.call-start = ((), (), s32[]{:S(2)}) async-start(), calls=%async_computation.6 | async-start | bytes 1310720 | tf_op jit(solution)/shard_map/all_gather | solution.py:63
  9.6 17.9 %copy-start.8 = (f32[256,512]{1,0:T(8,128)S(1)}, f32[256,512]{1,0:T(8,128)}, u32[]{:S(2)}) copy-start(f32[256,512]{1,0:T(8,128)} %param.31) | copy-start | bytes 1572868
  9.6 18.7 %all-to-all-start = ((f32[256,4,128]{2,0,1:T(8,128)}), f32[256,4,128]{2,0,1:T(8,128)S(1)}, u32[]{:S(2)}, u32[]{:S(2)}) async-start(f32[256,4,128]{2,0,1:T(8,128)} %copy_bitcast_fusion.1), calls=%async_computation | async-start | bytes 1048576 | tf_op jit(solution)/shard_map/all_to_all | solution.py:56
  14.0 12.1 %copy-start.9 = (f32[16,1024]{1,0:T(8,128)S(1)}, f32[16,1024]{1,0:T(8,128)}, u32[]{:S(2)}) copy-start(f32[16,1024]{1,0:T(8,128)} %param.37) | copy-start | bytes 196612
  14.0 113.8 %all-gather.9.cloned.1.call-start = ((), (), s32[]{:S(2)}) async-start(), calls=%async_computation.5 | async-start | bytes 1310720 | tf_op jit(solution)/shard_map/all_gather | solution.py:62
  14.5 0.7 copy-start.11
  26.0 0.7 copy-start.12
  28.3 178.7 %all-to-all-start.1 = ((f32[256,4,128]{2,0,1:T(8,128)}), f32[256,4,128]{2,0,1:T(8,128)}, u32[]{:S(2)}, u32[]{:S(2)}) async-start(f32[256,4,128]{2,0,1:T(8,128)} %copy_bitcast_fusion), calls=%async_computation.1 | async-start | bytes 1048576 | tf_op jit(solution)/shard_map/all_to_all | solution.py:57
  32.5 278.2 %reduce-scatter.4.cloned.1.call-start = ((), (), s32[]{:S(2)}) async-start(), calls=%async_computation.7 | async-start | bytes 655360
  32.6 16.6 %copy-start.13 = (s32[2]{0:T(128)S(1)}, s32[2]{0:T(128)}, u32[]{:S(2)}) copy-start(s32[2]{0:T(128)} %param.39) | copy-start | bytes 28
  57.3 15.5 %collective-permute-start.2 = (f32[1024,128]{1,0:T(8,128)S(1)}, f32[1024,128]{1,0:T(8,128)S(1)}, u32[]{:S(2)}, u32[]{:S(2)}) collective-permute-start(f32[1024,128]{1,0:T(8,128)S(1)} %get-tuple-element.1181), channel_id=1, source_target_pairs={{0,4},{4,8},{8,12},{1,5},{5,9},{9,13},{2,6},{6,10},{10,14},{3,7},{... | collective-permute-start | bytes 1572872 | tf_op jit(solution)/shard_map/while/body/eval_jaxpr/ppermute | solution.py:12
  81.0 15.1 %collective-permute-start.2 = (f32[1024,128]{1,0:T(8,128)S(1)}, f32[1024,128]{1,0:T(8,128)S(1)}, u32[]{:S(2)}, u32[]{:S(2)}) collective-permute-start(f32[1024,128]{1,0:T(8,128)S(1)} %get-tuple-element.1181), channel_id=1, source_target_pairs={{0,4},{4,8},{8,12},{1,5},{5,9},{9,13},{2,6},{6,10},{10,14},{3,7},{... | collective-permute-start | bytes 1572872 | tf_op jit(solution)/shard_map/while/body/eval_jaxpr/ppermute | solution.py:12
  104.3 14.2 %collective-permute-start.2 = (f32[1024,128]{1,0:T(8,128)S(1)}, f32[1024,128]{1,0:T(8,128)S(1)}, u32[]{:S(2)}, u32[]{:S(2)}) collective-permute-start(f32[1024,128]{1,0:T(8,128)S(1)} %get-tuple-element.1181), channel_id=1, source_target_pairs={{0,4},{4,8},{8,12},{1,5},{5,9},{9,13},{2,6},{6,10},{10,14},{3,7},{... | collective-permute-start | bytes 1572872 | tf_op jit(solution)/shard_map/while/body/eval_jaxpr/ppermute | solution.py:12
  118.6 1.2 copy-start.5
  121.1 1.2 copy-start.6
  125.1 1.2 copy-start.6
  127.8 1.2 copy-start.1
  136.9 14.1 %collective-permute-start = (f32[1024,128]{1,0:T(8,128)S(1)}, f32[1024,128]{1,0:T(8,128)S(1)}, u32[]{:S(2)}, u32[]{:S(2)}) collective-permute-start(f32[1024,128]{1,0:T(8,128)S(1)} %get-tuple-element.1225), channel_id=1, source_target_pairs={{4,0},{8,4},{12,8},{5,1},{9,5},{13,9},{6,2},{10,6},{14,10},{7,3},{... | collective-permute-start | bytes 1572872 | tf_op jit(solution)/shard_map/while/body/eval_jaxpr/ppermute | solution.py:12
  151.9 1.4 copy-start.1
  161.1 12.8 %collective-permute-start = (f32[1024,128]{1,0:T(8,128)S(1)}, f32[1024,128]{1,0:T(8,128)S(1)}, u32[]{:S(2)}, u32[]{:S(2)}) collective-permute-start(f32[1024,128]{1,0:T(8,128)S(1)} %get-tuple-element.1225), channel_id=1, source_target_pairs={{4,0},{8,4},{12,8},{5,1},{9,5},{13,9},{6,2},{10,6},{14,10},{7,3},{... | collective-permute-start | bytes 1572872 | tf_op jit(solution)/shard_map/while/body/eval_jaxpr/ppermute | solution.py:12
  174.8 1.4 copy-start.1
  184.1 11.9 %collective-permute-start = (f32[1024,128]{1,0:T(8,128)S(1)}, f32[1024,128]{1,0:T(8,128)S(1)}, u32[]{:S(2)}, u32[]{:S(2)}) collective-permute-start(f32[1024,128]{1,0:T(8,128)S(1)} %get-tuple-element.1225), channel_id=1, source_target_pairs={{4,0},{8,4},{12,8},{5,1},{9,5},{13,9},{6,2},{10,6},{14,10},{7,3},{... | collective-permute-start | bytes 1572872 | tf_op jit(solution)/shard_map/while/body/eval_jaxpr/ppermute | solution.py:12
  198.2 1.4 copy-start.7
  203.2 1.4 copy-start.7
  207.0 1.0 copy-start.4
  207.9 2.3 copy-start.2
  207.9 2.3 copy-start.3
  219.5 9.8 %collective-permute-start.1 = (f32[1024,128]{1,0:T(8,128)S(1)}, f32[1024,128]{1,0:T(8,128)}, u32[]{:S(2)}, u32[]{:S(2)}) collective-permute-start(f32[1024,128]{1,0:T(8,128)S(1)} %get-tuple-element.1207), channel_id=1, source_target_pairs={{0,4},{4,8},{8,12},{1,5},{5,9},{9,13},{2,6},{6,10},{10,14},{3,7},{... | collective-permute-start | bytes 1572872 | tf_op jit(solution)/shard_map/while/body/eval_jaxpr/ppermute | solution.py:12
  239.8 11.2 %collective-permute-start.1 = (f32[1024,128]{1,0:T(8,128)S(1)}, f32[1024,128]{1,0:T(8,128)}, u32[]{:S(2)}, u32[]{:S(2)}) collective-permute-start(f32[1024,128]{1,0:T(8,128)S(1)} %get-tuple-element.1207), channel_id=1, source_target_pairs={{0,4},{4,8},{8,12},{1,5},{5,9},{9,13},{2,6},{6,10},{10,14},{3,7},{... | collective-permute-start | bytes 1572872 | tf_op jit(solution)/shard_map/while/body/eval_jaxpr/ppermute | solution.py:12
  261.4 11.2 %collective-permute-start.1 = (f32[1024,128]{1,0:T(8,128)S(1)}, f32[1024,128]{1,0:T(8,128)}, u32[]{:S(2)}, u32[]{:S(2)}) collective-permute-start(f32[1024,128]{1,0:T(8,128)S(1)} %get-tuple-element.1207), channel_id=1, source_target_pairs={{0,4},{4,8},{8,12},{1,5},{5,9},{9,13},{2,6},{6,10},{10,14},{3,7},{... | collective-permute-start | bytes 1572872 | tf_op jit(solution)/shard_map/while/body/eval_jaxpr/ppermute | solution.py:12
  285.5 1.9 copy-start.10
Sparse Core Ops, SparseCore 0:
  8.9 20.9 all-gather.4
  31.5 17.6 all-gather.6
  50.8 17.6 all-gather.10
  69.9 16.6 all-gather.8
  288.6 22.0 reduce-scatter.3
where the time goes:
time: 321 us; the launch traced here: 319 us
  waiting for transfers between devices  126 us (39%)
  local copies, waits for them, and re-layouts  47.8 us (15%)
  starting transfers between devices  39.8 us (12%)
  matrix products  38.4 us (12%)
  loops' own time  26.9 us (8%)
  other arithmetic  15.8 us (5%)
  between operations  13.3 us (4%)
  blocking collectives  10.8 us (3%)
    ppermute x9, waiting for transfers between devices, passed_along(): lax.ppermute(value, axis, [(source, source + steps) for source in range(f...  84.5 us
    dynamic_slice x48, local copies, waits for them, and re-layouts, down_local(): lax.scan(down_step, source, (down_full, down_side, offsets))  32.5 us
    ppermute x9, starting transfers between devices, passed_along(): lax.ppermute(value, axis, [(source, source + steps) for source in range(f...  31.2 us
    unnamed x6, waiting for transfers between devices  24.9 us
    all_gather x1, waiting for transfers between devices, body(): lax.all_gather(down_off, 'harm', axis=1, tiled=True)  16.6 us
    another operation x4, loops' own time, adjoint_local(): lax.scan(adjoint_step, source, (up_full, up_side, offsets))  15.1 us
    dot_general x16, matrix products, band_apply(): jnp.einsum('ijk,ikw->ijw', off_blocks, rolled, precision=precise)  11 us
    all_gather x1, blocking collectives, body(): lax.all_gather(design, 'harm', axis=1, tiled=True)  10.8 us
  transfers between devices with their start and end apart: 16, of which 11 were waited for; matrix products, arithmetic and copies ran while one was open for 19% of the time, Pallas kernels for 0%

commit v1 on v0

--- a/solution.py
+++ b/solution.py
@@ -1,6 +1,10 @@
+import functools
+
 import jax
 import jax.numpy as jnp
 from jax import lax
+from jax.experimental import pallas as pl
+from jax.experimental.pallas import tpu as pltpu
 from jax.sharding import PartitionSpec as P
 
 precise = lax.Precision.HIGHEST
@@ -137,9 +141,367 @@
     return lax.psum_scatter(partial_terms, "harm", scatter_dimension=1, tiled=True)
 
 
+CHUNKS = 2
+BLOCK = 128
+NEAR = {0: 1, 3: 2}
+SITES = (1, 2)
+ACTIVE = pl.Squeezed()
+
+
+def moved(value, pairs):
+    flat = [(za * 4 + xa * 2 + ca, zb * 4 + xb * 2 + cb) for (za, xa, ca), (zb, xb, cb) in pairs]
+    return lax.ppermute(value, ("layer", "harm"), flat)
+
+
+def split_store(hl, value):
+    high = value.astype(jnp.bfloat16)
+    hl[:, :BLOCK] = high
+    hl[:, BLOCK:] = (value - high.astype(jnp.float32)).astype(jnp.bfloat16)
+
+
+def three_products(left_high, left_low, right, dims):
+    wide = lax.dot_general(left_high, right, dims, preferred_element_type=jnp.float32)
+    thin = lax.dot_general(left_low, right[:, :BLOCK], dims, preferred_element_type=jnp.float32)
+    return wide[:, :BLOCK] + (wide[:, BLOCK:] + thin)
+
+
+def block_rows(ref, at):
+    return ref[pl.ds(pl.multiple_of(at * BLOCK, BLOCK), BLOCK), :]
+
+
+def banded(wh, wl, hl, shift, blocks, emit):
+    dims = (((1,), (0,)), ((), ()))
+    for i in range(blocks):
+        j = lax.rem(i + shift, blocks)
+        rows = slice(i * BLOCK, (i + 1) * BLOCK)
+        right = jnp.concatenate([hl[rows, :], block_rows(hl, j)], axis=0)
+        emit(rows, three_products(wh[rows, :], wl[rows, :], right, dims))
+
+
+def banded_transpose(wh, wl, hl, shift, blocks, emit):
+    dims = (((0,), (0,)), ((), ()))
+    for j in range(blocks):
+        i = lax.rem(j - shift + blocks, blocks)
+        rows = slice(j * BLOCK, (j + 1) * BLOCK)
+        right = jnp.concatenate([hl[rows, :], block_rows(hl, i)], axis=0)
+        high = jnp.concatenate([wh[rows, :BLOCK], block_rows(wh, i)[:, BLOCK:]], axis=0)
+        low = jnp.concatenate([wl[rows, :BLOCK], block_rows(wl, i)[:, BLOCK:]], axis=0)
+        emit(rows, three_products(high, low, right, dims))
+
+
+def at_site(s, site, core):
+    return (s[0] == site) & (s[1] == core)
+
+
+def prep_kernel(core, s, *refs):
+    pieces, outs = refs[:8], refs[8:]
+    wh, wl = outs[0], outs[1]
+
+    @pl.when((s[1] == core) & ((s[0] == 1) | (s[0] == 2)))
+    def _():
+        inner_base = jnp.where(s[0] == 1, 2, 0)
+        for index, piece in enumerate(pieces):
+            base = inner_base if index < 4 else 2 - inner_base
+            side = s[2] if index % 4 < 2 else 1 - s[2]
+            lane = core if index % 2 == 0 else 1 - core
+            for l in range(2):
+                for r in range(2):
+                    top = l * 2 * BLOCK + r * BLOCK
+                    block = jnp.concatenate(
+                        [piece[top : top + BLOCK, :], piece[4 * BLOCK + top : 5 * BLOCK + top, :]], axis=1
+                    )
+                    high = block.astype(jnp.bfloat16)
+                    low = (block - high.astype(jnp.float32)).astype(jnp.bfloat16)
+                    at = side * 4 + lane * 2 + r
+                    rows = pl.ds(pl.multiple_of(at * BLOCK, BLOCK), BLOCK)
+                    wh[base + l, rows, :] = high
+                    wl[base + l, rows, :] = low
+                    if len(outs) > 2:
+                        row = piece[8 * BLOCK + 2 * l + r : 8 * BLOCK + 2 * l + r + 1, :]
+                        outs[2][base + l, rows, :] = jnp.transpose(jnp.broadcast_to(row, (BLOCK, BLOCK)))
+
+
+def down_kernel(site, blocks, last, s, field, wh, wl, stack, out, cur, hl):
+    l = pl.program_id(0)
+    steps = pl.num_programs(0)
+    active = at_site(s, site, 0)
+
+    @pl.when(active & (l == 0))
+    def _():
+        cur[...] = field[...]
+
+    @pl.when(active)
+    def _():
+        value = cur[...]
+        stack[...] = value
+        split_store(hl, value)
+
+    @pl.when(active & ((l < steps - 1) | last))
+    def _():
+        def emit(rows, value):
+            cur[rows, :] = value
+
+        banded(wh, wl, hl, s[3 + l], blocks, emit)
+
+    @pl.when(active & (l == steps - 1))
+    def _():
+        out[...] = cur[...]
+
+
+def up_kernel(site, blocks, top, s, *refs):
+    field = None if top else refs[0]
+    wh, wl, stack, mirror, out, cur, hl = refs[0 if top else 1 :]
+    l = pl.program_id(0)
+    steps = pl.num_programs(0)
+    active = at_site(s, site, 1)
+
+    @pl.when(active & (l == 0))
+    def _():
+        cur[...] = jnp.zeros_like(cur) if top else field[...]
+
+    @pl.when(active)
+    def _():
+        split_store(hl, cur[...])
+
+        def emit(rows, value):
+            cur[rows, :] = mirror[rows, :] * stack[rows, :] + value
+
+        banded(wh, wl, hl, s[3 + steps - 1 - l], blocks, emit)
+
+    @pl.when(active & (l == steps - 1))
+    def _():
+        out[...] = cur[...]
+
+
+def adjoint_kernel(site, blocks, total, s, *refs):
+    first = total is not None
+    field = refs[0]
+    wh, wl, stack, sums, out, cur, hl = refs[2 if first else 1 :]
+    l = pl.program_id(0)
+    steps = pl.num_programs(0)
+    active = at_site(s, site, 1)
+
+    @pl.when(active & (l == 0))
+    def _():
+        cur[...] = (field[...] - refs[1][...]) / total if first else field[...]
+
+    @pl.when(active)
+    def _():
+        split_store(hl, cur[...])
+        for i in range(blocks):
+            rows = slice(i * BLOCK, (i + 1) * BLOCK)
+            terms = jnp.transpose(cur[rows, :] * stack[rows, :])
+            sums[i : i + 1, :] = jnp.sum(terms, axis=0, keepdims=True)
+
+    @pl.when(active & ((l < steps - 1) | first))
+    def _():
+        def emit(rows, value):
+            cur[rows, :] = value
+
+        banded_transpose(wh, wl, hl, s[3 + l], blocks, emit)
+
+    @pl.when(active & (l == steps - 1))
+    def _():
+        out[...] = cur[...]
+
+
+def call(kernel, scalars, inputs, in_specs, out_shape, out_specs, grid, scratch=()):
+    return pl.pallas_call(
+        kernel,
+        out_shape=out_shape,
+        grid_spec=pltpu.PrefetchScalarGridSpec(
+            num_scalar_prefetch=1, grid=grid, in_specs=in_specs, out_specs=out_specs, scratch_shapes=list(scratch)
+        ),
+    )(scalars, *inputs)
+
+
+def whole(shape):
+    return pl.BlockSpec(shape, lambda l, s: (0,) * len(shape))
+
+
+def layer_block(steps, rows, width, reverse=False):
+    index = (lambda l, s: (steps - 1 - l, 0, 0)) if reverse else (lambda l, s: (l, 0, 0))
+    return pl.BlockSpec((ACTIVE, rows, width), index)
+
+
+def fast_body(
+    incident, target, down_diag, down_off, up_diag, up_off, design, profile, material, offsets
+):
+    rows_here, col_total = incident.shape
+    harm_total = rows_here * 4
+    blocks = harm_total // BLOCK
+    steps = 4
+    f32 = jnp.float32
+    here_z, here_h = lax.axis_index("layer"), lax.axis_index("harm")
+    here_x, here_c = here_h // 2, here_h % 2
+    onehot = (material[:, None] == jnp.arange(profile.shape[0], dtype=jnp.int32)[None, :]).astype(f32)
+    profile_here = lax.dynamic_slice_in_dim(profile, here_h * rows_here, rows_here, 1)
+    shape_rows = jnp.dot(onehot, profile_here, precision=precise)
+    reflect = design * shape_rows
+    extra = jnp.concatenate(
+        [
+            reflect.reshape(4, BLOCK),
+            jnp.broadcast_to(offsets.astype(f32)[:, None], (2, BLOCK)),
+            jnp.zeros((2, BLOCK), f32),
+        ],
+        axis=0,
+    )
+
+    def packed(diag, off):
+        return jnp.concatenate([diag.reshape(-1, BLOCK), off.reshape(-1, BLOCK), extra], axis=0)
+
+    zs, xs = range(4), range(2)
+
+    def gathered(core, own, swap_from):
+        swapped = moved(swap_from, [((z, x, 1 - core), (z, x, core)) for z in zs for x in xs])
+        over_x = lambda v, at: moved(v, [((z, x, core), (z, 1 - x, core)) for z in at for x in xs])
+        over_z = lambda v: moved(v, [((z, x, core), (n, x, core)) for z, n in NEAR.items() for x in xs])
+        if core:
+            own, swapped = lax.optimization_barrier((own, swapped))
+        beside_a = over_x(own, zs)
+        outer_a = over_z(own)
+        beside_b = over_x(swapped, SITES)
+        outer_b = over_z(swapped)
+        outer_beside_a = over_z(beside_a)
+        outer_beside_b = over_x(outer_b, SITES)
+        return [own, swapped, beside_a, beside_b, outer_a, outer_b, outer_beside_a, outer_beside_b]
+
+    def column_group(value, core, site):
+        chunk_cols = col_total // 2 // CHUNKS
+        part = lambda x: lax.dynamic_slice_in_dim(value, x * (col_total // 2), col_total // 2, 1)
+        cut = lambda v: v.reshape(rows_here, CHUNKS, chunk_cols).transpose(1, 0, 2)
+        mine, others = cut(part(here_x)), cut(part(1 - here_x))
+        partner = moved(mine, [((site, x, 1 - core), (site, x, core)) for x in xs])
+        beside = moved(others, [((site, x, core), (site, 1 - x, core)) for x in xs])
+        across = moved(others, [((site, x, 1 - core), (site, 1 - x, core)) for x in xs])
+        near = [mine, partner] if core == 0 else [partner, mine]
+        far = [beside, across] if core == 0 else [across, beside]
+        return jnp.where(here_x == 0, jnp.concatenate(near + far, 1), jnp.concatenate(far + near, 1))
+
+    down_pack = packed(down_diag, down_off)
+    up_pack = packed(up_diag, up_off)
+    down_pieces = gathered(0, down_pack, down_pack)
+    entry = column_group(incident, 0, 1)
+    up_pack_later, _ = lax.optimization_barrier((up_pack, down_pieces[5]))
+    up_pieces = gathered(1, up_pack, up_pack_later)
+    aim = column_group(target, 1, 1)
+
+    def scalars(pieces):
+        outer = pieces[4][8 * BLOCK + 4 : 8 * BLOCK + 6, 0].astype(jnp.int32)
+        turn = jnp.where(here_z < 2, jnp.concatenate([outer, offsets]), jnp.concatenate([offsets, outer]))
+        return jnp.concatenate([jnp.stack([here_z, here_c, here_x]), turn])
+
+    def prepared(core, pieces, scal):
+        weight = jax.ShapeDtypeStruct((steps, harm_total, 2 * BLOCK), jnp.bfloat16)
+        outs = [weight, weight] + ([jax.ShapeDtypeStruct((steps, harm_total, BLOCK), f32)] if core else [])
+        return call(
+            functools.partial(prep_kernel, core),
+            scal,
+            pieces,
+            [whole(p.shape) for p in pieces],
+            outs,
+            [whole(o.shape) for o in outs],
+            (1,),
+        )
+
+    down_scal, up_scal = scalars(down_pieces), scalars(up_pieces)
+    cols = col_total // 2 // CHUNKS
+    field_shape = jax.ShapeDtypeStruct((harm_total, cols), f32)
+    stack_shape = jax.ShapeDtypeStruct((steps, harm_total, cols), f32)
+    field_spec = whole((harm_total, cols))
+    scratch = [pltpu.VMEM((harm_total, cols), f32), pltpu.VMEM((harm_total, 2 * cols), jnp.bfloat16)]
+    weight_spec = layer_block(steps, harm_total, 2 * BLOCK)
+    stack_spec = layer_block(steps, harm_total, cols)
+    weight_back = layer_block(steps, harm_total, 2 * BLOCK, True)
+    stack_back = layer_block(steps, harm_total, cols, True)
+    dh, dl = prepared(0, down_pieces, down_scal)
+
+    def down_pass(site, field, last):
+        return call(
+            functools.partial(down_kernel, site, blocks, last),
+            down_scal,
+            [field, dh, dl],
+            [field_spec, weight_spec, weight_spec],
+            [stack_shape, field_shape],
+            [stack_spec, field_spec],
+            (steps,),
+            scratch,
+        )
+
+    to_two = lambda v, core: moved(v, [((1, x, core), (2, x, core)) for x in xs])
+    to_one = lambda v, core: moved(v, [((2, x, core), (1, x, core)) for x in xs])
+    chunks = range(CHUNKS)
+    stacks_one, handed = zip(*[down_pass(1, entry[k], True) for k in chunks])
+    received = [to_two(v, 0) for v in handed]
+    stacks_two = [down_pass(2, v, False)[0] for v in received]
+    share = lambda v, site: moved(v, [((site, x, 0), (site, x, 1)) for x in xs])
+    stacks_two = [share(v, 2) for v in stacks_two]
+    stacks_one = [share(v, 1) for v in stacks_one]
+    uh, ul, mirror = prepared(1, up_pieces, up_scal)
+
+    def up_pass(site, field, stack):
+        top = field is None
+        return call(
+            functools.partial(up_kernel, site, blocks, top),
+            up_scal,
+            ([] if top else [field]) + [uh, ul, stack, mirror],
+            ([] if top else [field_spec]) + [weight_back, weight_back, stack_back, stack_back],
+            field_shape,
+            field_spec,
+            (steps,),
+            scratch,
+        )
+
+    def adjoint_pass(site, fields, stack, total):
+        sums_shape = jax.ShapeDtypeStruct((steps, blocks, BLOCK), f32)
+        return call(
+            functools.partial(adjoint_kernel, site, blocks, total),
+            up_scal,
+            fields + [uh, ul, stack],
+            [field_spec] * len(fields) + [weight_spec, weight_spec, stack_spec],
+            [sums_shape, field_shape],
+            [layer_block(steps, blocks, BLOCK), field_spec],
+            (steps,),
+            scratch,
+        )
+
+    risen = [to_one(up_pass(2, None, stacks_two[k]), 1) for k in chunks]
+    sums_one, passed = [], []
+    for k in chunks:
+        reflected = up_pass(1, risen[k], stacks_one[k])
+        sums, adjoint = adjoint_pass(1, [reflected, aim[k]], stacks_one[k], float(col_total))
+        sums_one.append(sums)
+        passed.append(to_two(adjoint, 1))
+    sums_two = [adjoint_pass(2, [passed[k]], stacks_two[k], None)[0] for k in chunks]
+
+    half = blocks // 2
+    total_of = lambda parts: functools.reduce(jnp.add, parts)
+    part_of = lambda v, x: lax.dynamic_slice_in_dim(v, x * half, half, 1)
+
+    def finished(site, sums):
+        full = total_of(sums)
+        partner = moved(part_of(full, 1 - here_x), [((site, x, 1), (site, 1 - x, 1)) for x in xs])
+        mine = part_of(full, here_x) + partner
+        outer_at = 0 if site == 1 else 3
+        low, high = mine[:2], mine[2:]
+        inner, outer = (high, low) if site == 1 else (low, high)
+        a = moved(inner[:, :2], [((site, x, 1), (site, x, 0)) for x in xs])
+        b = moved(outer[:, :2], [((site, x, 1), (outer_at, x, 0)) for x in xs])
+        c = moved(outer[:, 2:], [((site, x, 1), (outer_at, x, 1)) for x in xs])
+        kept = jnp.where((here_z == site) & (here_c == 1), inner[:, 2:], 0.0)
+        return a + b + (c + kept)
+
+    total = finished(1, sums_one) + finished(2, sums_two)
+    return total.reshape(2, rows_here) * shape_rows
+
+
+def takes_fast_plan(mesh):
+    return mesh.shape["layer"] == 4 and mesh.shape["harm"] == 4
+
+
 def solution(mesh):
     return jax.shard_map(
-        body,
+        fast_body if takes_fast_plan(mesh) else body,
         mesh=mesh,
         in_specs=(
             P(("design", "harm"), None),

time: 321 us -> 209 us (0.65)
  Pallas kernels: 0 us -> 73.8 us
  waiting for transfers between devices: 126 us -> 52.7 us
  matrix products: 38.4 us -> 0.88 us
  local copies, waits for them, and re-layouts: 47.8 us -> 14 us
  loops' own time: 26.9 us -> 0 us
  starting transfers between devices: 39.8 us -> 57.5 us
  between operations: 13.3 us -> 0.64 us
  blocking collectives: 10.8 us -> 0 us
  other arithmetic: 15.8 us -> 7.01 us
    pallas_call x0 -> x14, Pallas kernels: none -> 73.8 us  [call(): pl.pallas_call(kernel, out_shape=out_shape, grid_spec=pltpu.PrefetchScala...]
    dot_general x49 -> x1, matrix products: 38.4 us -> 0.88 us  [fast_body(): shape_rows = jnp.dot(onehot, profile_here, precision=precise)]
    ppermute x9 -> x38, waiting for transfers between devices: 84.5 us -> 52.7 us  [moved(): return lax.ppermute(value, ('layer', 'harm'), flat)]
    dynamic_slice x56 -> x3, local copies, waits for them, and re-layouts: 32.5 us -> 1.28 us  [the longest x1 1.27 us: column_group(): lax.dynamic_slice_in_dim(value, x * (col_total // 2), col_total // 2, 1)]
    another operation x15 -> x0, loops' own time: 26.9 us -> none  [the longest x4 15.1 us: adjoint_local(): lax.scan(adjoint_step, source, (up_full, up_side, offsets))]
    ppermute x9 -> x38, starting transfers between devices: 31.2 us -> 57.5 us  [moved(): return lax.ppermute(value, ('layer', 'harm'), flat)]
    unnamed x6 -> x0, waiting for transfers between devices: 24.9 us -> none
    all_gather x4 -> x0, waiting for transfers between devices: 16.7 us -> none  [the longest x1 16.6 us: body(): lax.all_gather(down_off, 'harm', axis=1, tiled=True)]
  transfers between devices with their start and end apart: 16 -> 38, of which waited for: 11 -> 4; matrix products, arithmetic and copies ran while one was open for 19% -> 6% of each run, Pallas kernels for 0% -> 28%
where the time goes in v1:
time: 209 us; the launch traced here: 207 us
  Pallas kernels  73.8 us (35%)
  starting transfers between devices  57.5 us (28%)
  waiting for transfers between devices  52.7 us (25%)
  local copies, waits for them, and re-layouts  14 us (7%)
  other arithmetic  7.01 us (3%)
    pallas_call x14, Pallas kernels, call(): pl.pallas_call(kernel, out_shape=out_shape, grid_spec=pltpu.PrefetchScala...  73.8 us
    ppermute x38, starting transfers between devices, moved(): return lax.ppermute(value, ('layer', 'harm'), flat)  57.5 us
    ppermute x38, waiting for transfers between devices, moved(): return lax.ppermute(value, ('layer', 'harm'), flat)  52.7 us
    unnamed x40, local copies, waits for them, and re-layouts  5.43 us
  transfers between devices with their start and end apart: 38, of which 4 were waited for; matrix products, arithmetic and copies ran while one was open for 6% of the time, Pallas kernels for 28%

profile of v1, /device:TPU:0, one launch (start us, length us, event | category | flops | bytes accessed | tf_op | source)
XLA Modules:
  0.0 206.6 jit_solution(2783185736646114660)
XLA Ops:
  0.0 0.8 copy-done
  0.8 0.9 fusion.16
  2.5 2.0 concatenate.40.refs_0_
  4.4 1.3 collective-permute-start
  5.7 2.5 %collective-permute-done.refs_1_ = f32[1032,128]{1,0:T(8,128)S(1)} collective-permute-done((f32[1032,128]{1,0:T(8,128)S(1)}, f32[1032,128]{1,0:T(8,128)S(1)}, u32[]{:S(2)}, u32[]{:S(2)}) %collective-permute-start) | collective-permute-done | bytes 528416 | tf_op jit(solution)/shard_map/ppermute | solution.py:153
  8.2 5.8 %collective-permute-start.1 = (f32[1032,128]{1,0:T(8,128)S(1)}, f32[1032,128]{1,0:T(8,128)}, u32[]{:S(2)}, u32[]{:S(2)}) collective-permute-start(f32[1032,128]{1,0:T(8,128)S(1)} %collective-permute-done.refs_1_), channel_id=1, source_target_pairs={{0,4},{2,6},{12,8},{14,10},{16,20},{18,22},{28,24},{30,26}} | collective-permute-start | bytes 1585160 | tf_op jit(solution)/shard_map/ppermute | solution.py:153
  14.0 2.0 concatenate.39.refs_0_
  16.0 4.0 %collective-permute-done.1.refs_5_ = f32[1032,128]{1,0:T(8,128)} collective-permute-done((f32[1032,128]{1,0:T(8,128)S(1)}, f32[1032,128]{1,0:T(8,128)}, u32[]{:S(2)}, u32[]{:S(2)}) %collective-permute-start.1) | collective-permute-done | bytes 528416 | tf_op jit(solution)/shard_map/ppermute | solution.py:153
  19.9 1.3 collective-permute-start.2
  21.2 3.4 %collective-permute-start.13 = (f32[1032,128]{1,0:T(8,128)S(1)}, f32[1032,128]{1,0:T(8,128)}, u32[]{:S(2)}, u32[]{:S(2)}) collective-permute-start(f32[1032,128]{1,0:T(8,128)S(1)} %concatenate.40.refs_0_), channel_id=1, source_target_pairs={{0,2},{2,0},{4,6},{6,4},{8,10},{10,8},{12,14},{14,12},{16,18},{18,... | collective-permute-start | bytes 1585160 | tf_op jit(solution)/shard_map/ppermute | solution.py:153
  24.7 1.3 constant_dynamic-slice_fusion.3
  26.1 0.8 copy.14
  27.6 1.4 collective-permute-start.11
  29.2 0.7 collective-permute-start.10
  30.0 7.6 %collective-permute-start.9 = (f32[1032,128]{1,0:T(8,128)S(1)}, f32[1032,128]{1,0:T(8,128)}, u32[]{:S(2)}, u32[]{:S(2)}) collective-permute-start(f32[1032,128]{1,0:T(8,128)S(1)} %concatenate.40.refs_0_), channel_id=1, source_target_pairs={{0,4},{2,6},{12,8},{14,10},{16,20},{18,22},{28,24},{30,26}} | collective-permute-start | bytes 1585160 | tf_op jit(solution)/shard_map/ppermute | solution.py:153
  37.6 1.5 collective-permute-start.3
  39.1 1.2 maximum_select_fusion
  40.3 1.5 collective-permute-start.14
  41.8 6.3 %collective-permute-start.15 = (f32[1032,128]{1,0:T(8,128)}, f32[1032,128]{1,0:T(8,128)}, u32[]{:S(2)}, u32[]{:S(2)}) collective-permute-start(f32[1032,128]{1,0:T(8,128)} %collective-permute-done.13.refs_2_), channel_id=1, source_target_pairs={{0,4},{2,6},{12,8},{14,10},{16,20},{18,22},{28,24},{30,26}} | collective-permute-start | bytes 1585160 | tf_op jit(solution)/shard_map/ppermute | solution.py:153
  48.1 1.5 collective-permute-start.16
  49.5 1.0 slice_bitcast_fusion.1
  50.6 0.8 fusion.10
  51.4 0.8 fusion.11
  52.9 2.0 collective-permute-done.15.refs_6_
  54.9 4.8 %shard_map.101 = (bf16[4,1024,256]{2,1,0:T(8,128)(2,1)}, bf16[4,1024,256]{2,1,0:T(8,128)(2,1)}) custom-call(s32[7]{0:T(128)} %get-tuple-element.45.s, f32[1032,128]{1,0:T(8,128)} %copy-done.3, f32[1032,128]{1,0:T(8,128)} %copy-done.5, f32[1032,128]{1,0:T(8,128)} %collective-permute-done.13.refs_2_, f32[1032,128]{1,0:T(8,128)} %collective-permute-done.14.refs_3_, ...), custom_call_target="tpu_custom_call" | custom-call | tf_op jit(solution)/shard_map/pallas_call | solution.py:309
  59.7 5.1 %shard_map.102 = (f32[4,1024,128]{2,1,0:T(8,128)}, f32[1024,128]{1,0:T(8,128)}) custom-call(s32[7]{0:T(128)} %get-tuple-element.45.s, f32[1024,128]{1,0:T(8,128)} %get-tuple-element.50.field, bf16[4,1024,256]{2,1,0:T(8,128)(2,1)} %get-tuple-element.30.wh, bf16[4,1024,256]{2,1,0:T(8,128)(2,1)} %get-tuple-element.31.wl), custom_call_target="tpu_custom_call" | custom-call | tf_op jit(solution)/shard_map/pallas_call | solution.py:309
  64.8 0.7 collective-permute-start.17
  65.5 5.1 %shard_map.107 = (f32[4,1024,128]{2,1,0:T(8,128)}, f32[1024,128]{1,0:T(8,128)}) custom-call(s32[7]{0:T(128)} %get-tuple-element.45.s, f32[1024,128]{1,0:T(8,128)} %get-tuple-element.49.field, bf16[4,1024,256]{2,1,0:T(8,128)(2,1)} %get-tuple-element.30.wh, bf16[4,1024,256]{2,1,0:T(8,128)(2,1)} %get-tuple-element.31.wl), custom_call_target="tpu_custom_call" | custom-call | tf_op jit(solution)/shard_map/pallas_call | solution.py:309
  70.6 1.4 collective-permute-start.24
  72.0 0.8 copy-done.11
  72.9 5.1 %shard_map.103 = (f32[4,1024,128]{2,1,0:T(8,128)}, f32[1024,128]{1,0:T(8,128)}) custom-call(s32[7]{0:T(128)} %get-tuple-element.45.s, f32[1024,128]{1,0:T(8,128)} %copy-done.11, bf16[4,1024,256]{2,1,0:T(8,128)(2,1)} %get-tuple-element.30.wh, bf16[4,1024,256]{2,1,0:T(8,128)(2,1)} %get-tuple-element.31.wl), custom_call_target="tpu_custom_call" | custom-call | tf_op jit(solution)/shard_map/pallas_call | solution.py:309
  77.9 0.8 collective-permute-start.18
  79.0 0.7 collective-permute-start.23
  79.7 1.5 collective-permute-start.4
  81.2 1.4 collective-permute-start.5
  82.6 5.1 %shard_map.108 = (f32[4,1024,128]{2,1,0:T(8,128)}, f32[1024,128]{1,0:T(8,128)}) custom-call(s32[7]{0:T(128)} %get-tuple-element.45.s, f32[1024,128]{1,0:T(8,128)} %collective-permute-done.24.field, bf16[4,1024,256]{2,1,0:T(8,128)(2,1)} %get-tuple-element.30.wh, bf16[4,1024,256]{2,1,0:T(8,128)(2,1)} %get-tuple-element.31.wl), custom_call_target="tpu_custom_call" | custom-call | tf_op jit(solution)/shard_map/pallas_call | solution.py:309
  87.7 2.0 collective-permute-start.25
  89.7 0.7 collective-permute-start.6
  90.4 2.0 collective-permute-start.20
  92.4 2.0 collective-permute-start.27
  94.3 0.7 collective-permute-start.7
  95.1 0.7 collective-permute-start.8
  98.2 5.4 %shard_map.100 = (bf16[4,1024,256]{2,1,0:T(8,128)(2,1)}, bf16[4,1024,256]{2,1,0:T(8,128)(2,1)}, f32[4,1024,128]{2,1,0:T(8,128)}) custom-call(s32[7]{0:T(128)} %pad_add_fusion.s, f32[1032,128]{1,0:T(8,128)} %copy-done.2, f32[1032,128]{1,0:T(8,128)} %copy-done.4, f32[1032,128]{1,0:T(8,128)} %collective-permute-done.4.refs_2_, ...), custom_call_target="tpu_custom_call" | custom-call | tf_op jit(solution)/shard_map/pallas_call | solution.py:309
  103.6 5.3 %shard_map.104 = f32[1024,128]{1,0:T(8,128)} custom-call(s32[7]{0:T(128)} %pad_add_fusion.s, bf16[4,1024,256]{2,1,0:T(8,128)(2,1)} %get-tuple-element.28.refs_0_.refs_1_.refs_2_, bf16[4,1024,256]{2,1,0:T(8,128)(2,1)} %get-tuple-element.29.refs_1_.refs_2_.refs_3_, f32[4,1024,128]{2,1,0:T(8,128)} %copy-done.1, f32[4,1024,128]{2,1,0:T(8,128)} %get-tuple-element.34.refs_3_.refs_4_), custom_call_target="tpu_custom_call" | custom-call | tf_op jit(solution)/shard_map/pallas_call | solution.py:309
  108.9 0.7 collective-permute-start.19
  109.6 5.2 %shard_map.109 = f32[1024,128]{1,0:T(8,128)} custom-call(s32[7]{0:T(128)} %pad_add_fusion.s, bf16[4,1024,256]{2,1,0:T(8,128)(2,1)} %get-tuple-element.28.refs_0_.refs_1_.refs_2_, bf16[4,1024,256]{2,1,0:T(8,128)(2,1)} %get-tuple-element.29.refs_1_.refs_2_.refs_3_, f32[4,1024,128]{2,1,0:T(8,128)} %collective-permute-done.25.refs_2_.refs_3_, ...), custom_call_target="tpu_custom_call" | custom-call | tf_op jit(solution)/shard_map/pallas_call | solution.py:309
  114.9 0.7 collective-permute-start.26
  115.7 1.1 slice_bitcast_fusion
  116.8 0.8 copy-done.10
  117.6 5.5 %shard_map.105.refs_0_ = f32[1024,128]{1,0:T(8,128)} custom-call(s32[7]{0:T(128)} %pad_add_fusion.s, f32[1024,128]{1,0:T(8,128)} %copy-done.10, bf16[4,1024,256]{2,1,0:T(8,128)(2,1)} %get-tuple-element.28.refs_0_.refs_1_.refs_2_, bf16[4,1024,256]{2,1,0:T(8,128)(2,1)} %get-tuple-element.29.refs_1_.refs_2_.refs_3_, ...), custom_call_target="tpu_custom_call" | custom-call | tf_op jit(solution)/shard_map/pallas_call | solution.py:309
  123.1 5.4 %shard_map.106 = (f32[4,8,128]{2,1,0:T(8,128)}, f32[1024,128]{1,0:T(8,128)}) custom-call(s32[7]{0:T(128)} %pad_add_fusion.s, f32[1024,128]{1,0:T(8,128)} %shard_map.105.refs_0_, f32[1024,128]{1,0:T(8,128)} %get-tuple-element.48.refs_1_, bf16[4,1024,256]{2,1,0:T(8,128)(2,1)} %get-tuple-element.28.refs_0_.refs_1_.refs_2_, ...), custom_call_target="tpu_custom_call" | custom-call | tf_op jit(solution)/shard_map/pallas_call | solution.py:309
  128.4 0.9 collective-permute-start.32
  129.4 0.8 copy-done.9
  130.1 5.5 %shard_map.110.refs_0_ = f32[1024,128]{1,0:T(8,128)} custom-call(s32[7]{0:T(128)} %pad_add_fusion.s, f32[1024,128]{1,0:T(8,128)} %copy-done.9, bf16[4,1024,256]{2,1,0:T(8,128)(2,1)} %get-tuple-element.28.refs_0_.refs_1_.refs_2_, bf16[4,1024,256]{2,1,0:T(8,128)(2,1)} %get-tuple-element.29.refs_1_.refs_2_.refs_3_, ...), custom_call_target="tpu_custom_call" | custom-call | tf_op jit(solution)/shard_map/pallas_call | solution.py:309
  135.7 5.5 %shard_map.111 = (f32[4,8,128]{2,1,0:T(8,128)}, f32[1024,128]{1,0:T(8,128)}) custom-call(s32[7]{0:T(128)} %pad_add_fusion.s, f32[1024,128]{1,0:T(8,128)} %shard_map.110.refs_0_, f32[1024,128]{1,0:T(8,128)} %get-tuple-element.47.refs_1_, bf16[4,1024,256]{2,1,0:T(8,128)(2,1)} %get-tuple-element.28.refs_0_.refs_1_.refs_2_, ...), custom_call_target="tpu_custom_call" | custom-call | tf_op jit(solution)/shard_map/pallas_call | solution.py:309
  141.2 0.7 collective-permute-start.33
  141.9 0.7 add.61
  143.3 0.8 copy-done.12
  144.1 5.4 %shard_map.112 = (f32[4,8,128]{2,1,0:T(8,128)}, f32[1024,128]{1,0:T(8,128)}) custom-call(s32[7]{0:T(128)} %pad_add_fusion.s, f32[1024,128]{1,0:T(8,128)} %copy-done.12, bf16[4,1024,256]{2,1,0:T(8,128)(2,1)} %get-tuple-element.28.refs_0_.refs_1_.refs_2_, bf16[4,1024,256]{2,1,0:T(8,128)(2,1)} %get-tuple-element.29.refs_1_.refs_2_.refs_3_, ...), custom_call_target="tpu_custom_call" | custom-call | tf_op jit(solution)/shard_map/pallas_call | solution.py:309
  149.5 0.8 copy-done.13
  150.3 5.4 %shard_map.113 = (f32[4,8,128]{2,1,0:T(8,128)}, f32[1024,128]{1,0:T(8,128)}) custom-call(s32[7]{0:T(128)} %pad_add_fusion.s, f32[1024,128]{1,0:T(8,128)} %copy-done.13, bf16[4,1024,256]{2,1,0:T(8,128)(2,1)} %get-tuple-element.28.refs_0_.refs_1_.refs_2_, bf16[4,1024,256]{2,1,0:T(8,128)(2,1)} %get-tuple-element.29.refs_1_.refs_2_.refs_3_, ...), custom_call_target="tpu_custom_call" | custom-call | tf_op jit(solution)/shard_map/pallas_call | solution.py:309
  155.7 0.7 add.68
  158.4 1.3 collective-permute-start.30
  161.8 44.2 %collective-permute-done.30 = f32[2,2,128]{2,1,0:T(2,128)S(1)} collective-permute-done((f32[2,2,128]{2,1,0:T(2,128)S(1)}, f32[2,2,128]{2,1,0:T(2,128)S(1)}, u32[]{:S(2)}, u32[]{:S(2)}) %collective-permute-start.30) | collective-permute-done | bytes 2080 | tf_op jit(solution)/shard_map/ppermute | solution.py:153
  (97 shorter events, 10.7 us)
Async XLA Ops:
  0.0 0.8 copy-start
  4.4 25.5 %copy-start.3 = (f32[1032,128]{1,0:T(8,128)}, f32[1032,128]{1,0:T(8,128)S(1)}, u32[]{:S(2)}) copy-start(f32[1032,128]{1,0:T(8,128)S(1)} %concatenate.40.refs_0_) | copy-start | bytes 1585156
  4.4 3.8 %collective-permute-start = (f32[1032,128]{1,0:T(8,128)S(1)}, f32[1032,128]{1,0:T(8,128)S(1)}, u32[]{:S(2)}, u32[]{:S(2)}) collective-permute-start(f32[1032,128]{1,0:T(8,128)S(1)} %concatenate.40.refs_0_), channel_id=1, source_target_pairs={{1,0},{3,2},{5,4},{7,6},{9,8},{11,10},{13,12},{15,14},{17,16},{19,... | collective-permute-start | bytes 1585160 | tf_op jit(solution)/shard_map/ppermute | solution.py:153
  8.2 7.7 %copy-start.5 = (f32[1032,128]{1,0:T(8,128)}, f32[1032,128]{1,0:T(8,128)S(1)}, u32[]{:S(2)}) copy-start(f32[1032,128]{1,0:T(8,128)S(1)} %collective-permute-done.refs_1_) | copy-start | bytes 1585156
  8.2 11.7 %collective-permute-start.1 = (f32[1032,128]{1,0:T(8,128)S(1)}, f32[1032,128]{1,0:T(8,128)}, u32[]{:S(2)}, u32[]{:S(2)}) collective-permute-start(f32[1032,128]{1,0:T(8,128)S(1)} %collective-permute-done.refs_1_), channel_id=1, source_target_pairs={{0,4},{2,6},{12,8},{14,10},{16,20},{18,22},{28,24},{30,26}} | collective-permute-start | bytes 1585160 | tf_op jit(solution)/shard_map/ppermute | solution.py:153
  16.0 63.7 %copy-start.2 = (f32[1032,128]{1,0:T(8,128)}, f32[1032,128]{1,0:T(8,128)S(1)}, u32[]{:S(2)}) copy-start(f32[1032,128]{1,0:T(8,128)S(1)} %concatenate.39.refs_0_) | copy-start | bytes 1585156
  19.9 10.0 %collective-permute-start.2 = (f32[1032,128]{1,0:T(8,128)S(1)}, f32[1032,128]{1,0:T(8,128)S(1)}, u32[]{:S(2)}, u32[]{:S(2)}) collective-permute-start(f32[1032,128]{1,0:T(8,128)S(1)} %concatenate.39.refs_0_), channel_id=1, source_target_pairs={{0,1},{2,3},{4,5},{6,7},{8,9},{10,11},{12,13},{14,15},{16,17},{18,... | collective-permute-start | bytes 1585160 | tf_op jit(solution)/shard_map/ppermute | solution.py:153
  21.2 20.5 %collective-permute-start.13 = (f32[1032,128]{1,0:T(8,128)S(1)}, f32[1032,128]{1,0:T(8,128)}, u32[]{:S(2)}, u32[]{:S(2)}) collective-permute-start(f32[1032,128]{1,0:T(8,128)S(1)} %concatenate.40.refs_0_), channel_id=1, source_target_pairs={{0,2},{2,0},{4,6},{6,4},{8,10},{10,8},{12,14},{14,12},{16,18},{18,... | collective-permute-start | bytes 1585160 | tf_op jit(solution)/shard_map/ppermute | solution.py:153
  26.9 10.7 %collective-permute-start.12 = (f32[2,256,128]{2,1,0:T(8,128)}, f32[2,256,128]{2,1,0:T(8,128)S(1)}, u32[]{:S(2)}, u32[]{:S(2)}) collective-permute-start(f32[2,256,128]{2,1,0:T(8,128)} %bitcast.10), channel_id=1, source_target_pairs={{5,6},{7,4},{21,22},{23,20}} | collective-permute-start | bytes 786440 | tf_op jit(solution)/shard_map/ppermute | solution.py:153
  27.6 11.5 %collective-permute-start.11 = (f32[2,256,128]{2,1,0:T(8,128)}, f32[2,256,128]{2,1,0:T(8,128)}, u32[]{:S(2)}, u32[]{:S(2)}) collective-permute-start(f32[2,256,128]{2,1,0:T(8,128)} %bitcast.10), channel_id=1, source_target_pairs={{4,6},{6,4},{20,22},{22,20}} | collective-permute-start | bytes 786440 | tf_op jit(solution)/shard_map/ppermute | solution.py:153
  29.2 9.8 %collective-permute-start.10 = (f32[2,256,128]{2,1,0:T(8,128)S(1)}, f32[2,256,128]{2,1,0:T(8,128)S(1)}, u32[]{:S(2)}, u32[]{:S(2)}) collective-permute-start(f32[2,256,128]{2,1,0:T(8,128)S(1)} %bitcast.29), channel_id=1, source_target_pairs={{5,4},{7,6},{21,20},{23,22}} | collective-permute-start | bytes 786440 | tf_op jit(solution)/shard_map/ppermute | solution.py:153
  30.0 34.9 %copy-start.4 = (f32[1032,128]{1,0:T(8,128)}, f32[1032,128]{1,0:T(8,128)S(1)}, u32[]{:S(2)}) copy-start(f32[1032,128]{1,0:T(8,128)S(1)} %collective-permute-done.2.refs_1_) | copy-start | bytes 1585156
  30.0 20.6 %collective-permute-start.9 = (f32[1032,128]{1,0:T(8,128)S(1)}, f32[1032,128]{1,0:T(8,128)}, u32[]{:S(2)}, u32[]{:S(2)}) collective-permute-start(f32[1032,128]{1,0:T(8,128)S(1)} %concatenate.40.refs_0_), channel_id=1, source_target_pairs={{0,4},{2,6},{12,8},{14,10},{16,20},{18,22},{28,24},{30,26}} | collective-permute-start | bytes 1585160 | tf_op jit(solution)/shard_map/ppermute | solution.py:153
  37.6 13.8 %collective-permute-start.3 = (f32[1032,128]{1,0:T(8,128)S(1)}, f32[1032,128]{1,0:T(8,128)}, u32[]{:S(2)}, u32[]{:S(2)}) collective-permute-start(f32[1032,128]{1,0:T(8,128)S(1)} %concatenate.39.refs_0_), channel_id=1, source_target_pairs={{1,5},{3,7},{13,9},{15,11},{17,21},{19,23},{29,25},{31,27}} | collective-permute-start | bytes 1585160 | tf_op jit(solution)/shard_map/ppermute | solution.py:153
  39.1 13.1 %copy-start.17 = (s32[2]{0:T(128)S(1)}, s32[2]{0:T(128)}, u32[]{:S(2)}) copy-start(s32[2]{0:T(128)} %param.19) | copy-start | bytes 28
  40.3 12.6 %collective-permute-start.14 = (f32[1032,128]{1,0:T(8,128)}, f32[1032,128]{1,0:T(8,128)}, u32[]{:S(2)}, u32[]{:S(2)}) collective-permute-start(f32[1032,128]{1,0:T(8,128)} %copy-done.5), channel_id=1, source_target_pairs={{4,6},{6,4},{8,10},{10,8},{20,22},{22,20},{24,26},{26,24}} | collective-permute-start | bytes 1585160 | tf_op jit(solution)/shard_map/ppermute | solution.py:153
  41.8 13.1 %collective-permute-start.15 = (f32[1032,128]{1,0:T(8,128)}, f32[1032,128]{1,0:T(8,128)}, u32[]{:S(2)}, u32[]{:S(2)}) collective-permute-start(f32[1032,128]{1,0:T(8,128)} %collective-permute-done.13.refs_2_), channel_id=1, source_target_pairs={{0,4},{2,6},{12,8},{14,10},{16,20},{18,22},{28,24},{30,26}} | collective-permute-start | bytes 1585160 | tf_op jit(solution)/shard_map/ppermute | solution.py:153
  48.1 6.8 %collective-permute-start.16 = (f32[1032,128]{1,0:T(8,128)}, f32[1032,128]{1,0:T(8,128)}, u32[]{:S(2)}, u32[]{:S(2)}) collective-permute-start(f32[1032,128]{1,0:T(8,128)} %collective-permute-done.1.refs_5_), channel_id=1, source_target_pairs={{4,6},{6,4},{8,10},{10,8},{20,22},{22,20},{24,26},{26,24}} | collective-permute-start | bytes 1585160 | tf_op jit(solution)/shard_map/ppermute | solution.py:153
  64.8 7.2 %collective-permute-start.17 = (f32[1024,128]{1,0:T(8,128)}, f32[1024,128]{1,0:T(8,128)S(1)}, u32[]{:S(2)}, u32[]{:S(2)}) collective-permute-start(f32[1024,128]{1,0:T(8,128)} %get-tuple-element.32), channel_id=1, source_target_pairs={{4,8},{6,10},{20,24},{22,26}} | collective-permute-start | bytes 1572872 | tf_op jit(solution)/shard_map/ppermute | solution.py:153
  70.6 12.0 %collective-permute-start.24 = (f32[1024,128]{1,0:T(8,128)}, f32[1024,128]{1,0:T(8,128)}, u32[]{:S(2)}, u32[]{:S(2)}) collective-permute-start(f32[1024,128]{1,0:T(8,128)} %get-tuple-element.37), channel_id=1, source_target_pairs={{4,8},{6,10},{20,24},{22,26}} | collective-permute-start | bytes 1572872 | tf_op jit(solution)/shard_map/ppermute | solution.py:153
  72.0 0.8 copy-start.11
  77.9 18.9 %collective-permute-start.18 = (f32[4,1024,128]{2,1,0:T(8,128)}, f32[4,1024,128]{2,1,0:T(8,128)S(1)}, u32[]{:S(2)}, u32[]{:S(2)}) collective-permute-start(f32[4,1024,128]{2,1,0:T(8,128)} %get-tuple-element.33), channel_id=1, source_target_pairs={{8,9},{10,11},{24,25},{26,27}} | collective-permute-start | bytes 6291464 | tf_op jit(solution)/shard_map/ppermute | solution.py:153
  79.0 8.7 %copy-start.14 = (f32[256,2,128]{2,0,1:T(8,128)}, f32[256,2,128]{2,0,1:T(8,128)S(1)}, u32[]{:S(2)}) copy-start(f32[256,2,128]{2,0,1:T(8,128)S(1)} %copy.18) | copy-start | bytes 786436
  79.0 10.7 %collective-permute-start.23 = (f32[2,256,128]{2,1,0:T(8,128)S(1)}, f32[2,256,128]{2,1,0:T(8,128)S(1)}, u32[]{:S(2)}, u32[]{:S(2)}) collective-permute-start(f32[2,256,128]{2,1,0:T(8,128)S(1)} %bitcast.35), channel_id=1, source_target_pairs={{5,7},{7,5},{21,23},{23,21}} | collective-permute-start | bytes 786440 | tf_op jit(solution)/shard_map/ppermute | solution.py:153
  79.7 10.7 %collective-permute-start.4 = (f32[1032,128]{1,0:T(8,128)S(1)}, f32[1032,128]{1,0:T(8,128)}, u32[]{:S(2)}, u32[]{:S(2)}) collective-permute-start(f32[1032,128]{1,0:T(8,128)S(1)} %concatenate.39.refs_0_), channel_id=1, source_target_pairs={{1,3},{3,1},{5,7},{7,5},{9,11},{11,9},{13,15},{15,13},{17,19},{19,... | collective-permute-start | bytes 1585160 | tf_op jit(solution)/shard_map/ppermute | solution.py:153
  81.2 11.2 %collective-permute-start.5 = (f32[1032,128]{1,0:T(8,128)}, f32[1032,128]{1,0:T(8,128)}, u32[]{:S(2)}, u32[]{:S(2)}) collective-permute-start(f32[1032,128]{1,0:T(8,128)} %copy-done.4), channel_id=1, source_target_pairs={{5,7},{7,5},{9,11},{11,9},{21,23},{23,21},{25,27},{27,25}} | collective-permute-start | bytes 1585160 | tf_op jit(solution)/shard_map/ppermute | solution.py:153
  87.7 21.2 %collective-permute-start.25 = (f32[4,1024,128]{2,1,0:T(8,128)}, f32[4,1024,128]{2,1,0:T(8,128)}, u32[]{:S(2)}, u32[]{:S(2)}) collective-permute-start(f32[4,1024,128]{2,1,0:T(8,128)} %get-tuple-element.38), channel_id=1, source_target_pairs={{8,9},{10,11},{24,25},{26,27}} | collective-permute-start | bytes 6291464 | tf_op jit(solution)/shard_map/ppermute | solution.py:153
  89.7 4.6 %collective-permute-start.6 = (f32[1032,128]{1,0:T(8,128)}, f32[1032,128]{1,0:T(8,128)S(1)}, u32[]{:S(2)}, u32[]{:S(2)}) collective-permute-start(f32[1032,128]{1,0:T(8,128)} %copy-done.4), channel_id=1, source_target_pairs={{1,5},{3,7},{13,9},{15,11},{17,21},{19,23},{29,25},{31,27}} | collective-permute-start | bytes 1585160 | tf_op jit(solution)/shard_map/ppermute | solution.py:153
  90.4 26.3 %collective-permute-start.20 = (f32[4,1024,128]{2,1,0:T(8,128)}, f32[4,1024,128]{2,1,0:T(8,128)}, u32[]{:S(2)}, u32[]{:S(2)}) collective-permute-start(f32[4,1024,128]{2,1,0:T(8,128)} %get-tuple-element.35), channel_id=1, source_target_pairs={{4,5},{6,7},{20,21},{22,23}} | collective-permute-start | bytes 6291464 | tf_op jit(solution)/shard_map/ppermute | solution.py:153
  92.4 36.9 %collective-permute-start.27 = (f32[4,1024,128]{2,1,0:T(8,128)}, f32[4,1024,128]{2,1,0:T(8,128)}, u32[]{:S(2)}, u32[]{:S(2)}) collective-permute-start(f32[4,1024,128]{2,1,0:T(8,128)} %get-tuple-element.39), channel_id=1, source_target_pairs={{4,5},{6,7},{20,21},{22,23}} | collective-permute-start | bytes 6291464 | tf_op jit(solution)/shard_map/ppermute | solution.py:153
  94.3 2.1 %copy-start.6 = (f32[1032,128]{1,0:T(8,128)}, f32[1032,128]{1,0:T(8,128)S(1)}, u32[]{:S(2)}) copy-start(f32[1032,128]{1,0:T(8,128)S(1)} %collective-permute-done.6.refs_5_) | copy-start | bytes 1585156
  94.3 0.7 collective-permute-start.7
  95.0 1.4 copy-start.7
  95.1 0.7 collective-permute-start.8
  95.8 0.8 copy-start.8
  95.8 19.1 %collective-permute-start.22 = (f32[2,256,128]{2,1,0:T(8,128)}, f32[2,256,128]{2,1,0:T(8,128)S(1)}, u32[]{:S(2)}, u32[]{:S(2)}) collective-permute-start(f32[2,256,128]{2,1,0:T(8,128)} %bitcast.36), channel_id=1, source_target_pairs={{4,7},{6,5},{20,23},{22,21}} | collective-permute-start | bytes 786440 | tf_op jit(solution)/shard_map/ppermute | solution.py:153
  96.9 6.8 %copy-start.1 = (f32[4,1024,128]{2,1,0:T(8,128)}, f32[4,1024,128]{2,1,0:T(8,128)S(1)}, u32[]{:S(2)}) copy-start(f32[4,1024,128]{2,1,0:T(8,128)S(1)} %collective-permute-done.18.refs_2_.refs_3_) | copy-start | bytes 6291460
  96.9 18.7 %collective-permute-start.21 = (f32[2,256,128]{2,1,0:T(8,128)S(1)}, f32[2,256,128]{2,1,0:T(8,128)S(1)}, u32[]{:S(2)}, u32[]{:S(2)}) collective-permute-start(f32[2,256,128]{2,1,0:T(8,128)S(1)} %bitcast.27), channel_id=1, source_target_pairs={{4,5},{6,7},{20,21},{22,23}} | collective-permute-start | bytes 786440 | tf_op jit(solution)/shard_map/ppermute | solution.py:153
  108.9 7.8 %collective-permute-start.19 = (f32[1024,128]{1,0:T(8,128)}, f32[1024,128]{1,0:T(8,128)S(1)}, u32[]{:S(2)}, u32[]{:S(2)}) collective-permute-start(f32[1024,128]{1,0:T(8,128)} %shard_map.104), channel_id=1, source_target_pairs={{9,5},{11,7},{25,21},{27,23}} | collective-permute-start | bytes 1572872 | tf_op jit(solution)/shard_map/ppermute | solution.py:153
  114.9 14.5 %collective-permute-start.26 = (f32[1024,128]{1,0:T(8,128)}, f32[1024,128]{1,0:T(8,128)S(1)}, u32[]{:S(2)}, u32[]{:S(2)}) collective-permute-start(f32[1024,128]{1,0:T(8,128)} %shard_map.109), channel_id=1, source_target_pairs={{9,5},{11,7},{25,21},{27,23}} | collective-permute-start | bytes 1572872 | tf_op jit(solution)/shard_map/ppermute | solution.py:153
  116.8 0.8 copy-start.10
  128.4 14.9 %collective-permute-start.32 = (f32[1024,128]{1,0:T(8,128)}, f32[1024,128]{1,0:T(8,128)S(1)}, u32[]{:S(2)}, u32[]{:S(2)}) collective-permute-start(f32[1024,128]{1,0:T(8,128)} %get-tuple-element.41), channel_id=1, source_target_pairs={{5,9},{7,11},{21,25},{23,27}} | collective-permute-start | bytes 1572872 | tf_op jit(solution)/shard_map/ppermute | solution.py:153
  129.3 0.8 copy-start.9
  135.7 6.2 %copy-start.15 = (f32[4,8,128]{2,1,0:T(8,128)S(1)}, f32[4,8,128]{2,1,0:T(8,128)}, u32[]{:S(2)}) copy-start(f32[4,8,128]{2,1,0:T(8,128)} %get-tuple-element.36) | copy-start | bytes 49156
  141.2 8.3 %collective-permute-start.33 = (f32[1024,128]{1,0:T(8,128)}, f32[1024,128]{1,0:T(8,128)S(1)}, u32[]{:S(2)}, u32[]{:S(2)}) collective-permute-start(f32[1024,128]{1,0:T(8,128)} %get-tuple-element.43), channel_id=1, source_target_pairs={{5,9},{7,11},{21,25},{23,27}} | collective-permute-start | bytes 1572872 | tf_op jit(solution)/shard_map/ppermute | solution.py:153
  142.6 0.7 collective-permute-start.28
  143.3 0.8 copy-start.12
  149.5 6.2 %copy-start.16 = (f32[4,8,128]{2,1,0:T(8,128)S(1)}, f32[4,8,128]{2,1,0:T(8,128)}, u32[]{:S(2)}) copy-start(f32[4,8,128]{2,1,0:T(8,128)} %get-tuple-element.42) | copy-start | bytes 49156
  149.5 0.8 copy-start.13
  156.4 3.3 %collective-permute-start.34 = (f32[4,4,128]{2,1,0:T(4,128)S(1)}, f32[4,4,128]{2,1,0:T(4,128)S(1)}, u32[]{:S(2)}, u32[]{:S(2)}) collective-permute-start(f32[4,4,128]{2,1,0:T(4,128)S(1)} %constant_dynamic-slice_fusion), channel_id=1, source_target_pairs={{9,11},{11,9},{25,27},{27,25}} | collective-permute-start | bytes 24584 | tf_op jit(solution)/shard_map/ppermute | solution.py:153
  157.1 4.0 %collective-permute-start.31 = (f32[2,2,128]{2,1,0:T(2,128)S(1)}, f32[2,2,128]{2,1,0:T(2,128)S(1)}, u32[]{:S(2)}, u32[]{:S(2)}) collective-permute-start(f32[2,2,128]{2,1,0:T(2,128)S(1)} %get-tuple-element.56), channel_id=1, source_target_pairs={{5,1},{7,3},{21,17},{23,19}} | collective-permute-start | bytes 6152 | tf_op jit(solution)/shard_map/ppermute | solution.py:153
  157.8 4.0 %collective-permute-start.29 = (f32[2,2,128]{2,1,0:T(2,128)S(1)}, f32[2,2,128]{2,1,0:T(2,128)S(1)}, u32[]{:S(2)}, u32[]{:S(2)}) collective-permute-start(f32[2,2,128]{2,1,0:T(2,128)S(1)} %get-tuple-element.57), channel_id=1, source_target_pairs={{5,4},{7,6},{21,20},{23,22}} | collective-permute-start | bytes 6152 | tf_op jit(solution)/shard_map/ppermute | solution.py:153
  158.4 47.6 %collective-permute-start.30 = (f32[2,2,128]{2,1,0:T(2,128)S(1)}, f32[2,2,128]{2,1,0:T(2,128)S(1)}, u32[]{:S(2)}, u32[]{:S(2)}) collective-permute-start(f32[2,2,128]{2,1,0:T(2,128)S(1)} %get-tuple-element.55), channel_id=1, source_target_pairs={{5,0},{7,2},{21,16},{23,18}} | collective-permute-start | bytes 6152 | tf_op jit(solution)/shard_map/ppermute | solution.py:153
  159.8 46.2 %collective-permute-start.37 = (f32[2,2,128]{2,1,0:T(2,128)S(1)}, f32[2,2,128]{2,1,0:T(2,128)S(1)}, u32[]{:S(2)}, u32[]{:S(2)}) collective-permute-start(f32[2,2,128]{2,1,0:T(2,128)S(1)} %get-tuple-element.59), channel_id=1, source_target_pairs={{9,13},{11,15},{25,29},{27,31}} | collective-permute-start | bytes 6152 | tf_op jit(solution)/shard_map/ppermute | solution.py:153
  160.4 45.6 %collective-permute-start.35 = (f32[2,2,128]{2,1,0:T(2,128)S(1)}, f32[2,2,128]{2,1,0:T(2,128)S(1)}, u32[]{:S(2)}, u32[]{:S(2)}) collective-permute-start(f32[2,2,128]{2,1,0:T(2,128)S(1)} %get-tuple-element.60), channel_id=1, source_target_pairs={{9,8},{11,10},{25,24},{27,26}} | collective-permute-start | bytes 6152 | tf_op jit(solution)/shard_map/ppermute | solution.py:153
  161.1 44.9 %collective-permute-start.36 = (f32[2,2,128]{2,1,0:T(2,128)S(1)}, f32[2,2,128]{2,1,0:T(2,128)S(1)}, u32[]{:S(2)}, u32[]{:S(2)}) collective-permute-start(f32[2,2,128]{2,1,0:T(2,128)S(1)} %get-tuple-element.58), channel_id=1, source_target_pairs={{9,12},{11,14},{25,28},{27,30}} | collective-permute-start | bytes 6152 | tf_op jit(solution)/shard_map/ppermute | solution.py:153
